TPU v7x, 256 devices: a whole 4x4x8 slice. The times are simulated.
256 devices in a mesh: region: 32 (over x, z), comm: 8 (over y, core).
Axes of the slice: x: 4, y: 4, z: 8, core: 2. Of those that a mesh axis runs over, the one named last changes fastest.
Arguments:
- cost: float32 [128, 262144], P('comm', 'region'), may hold values from 0.01 to 15, as said below
- flow_start: float32 [128, 262144], P('comm', 'region'), may hold values from 0 to 0.5
- capacity: float32 [262144], P('region'), may hold values from 5 to 135, as said below
- cap_dual_start: float32 [262144], P('region'), may hold values from 0 to 1
- demand: float32 [128, 131072], P('comm', 'region'), may hold values from -24 to 24
- node_dual_start: float32 [128, 131072], P('comm', 'region'), may hold values from -6 to 6
- incidence: float32 [4096, 128, 128], P('region'), may hold values from -0.25 to 0.25
- block_node: int32 [4096], P('region'), may hold values from 0 to 39
- ghost_source: int32 [256], P('region'), may hold values from 0 to 127, as said below
Outputs:
- final_flow: float32 [128, 262144], P('comm', 'region')
- final_cap_dual: float32 [262144], P('region')
- final_node_dual: float32 [128, 131072], P('comm', 'region')
Inputs may be any that keep to these rules, and one draw needn't show every extreme that they name: Each cost is positive. Each capacity is positive. `ghost_source`: ghost slot g of region r names boundary block j of region q as q * 4 + j. Slot 0 of every region has q = r + 16 in cyclic order; every other slot has q at most two regions from r in cyclic order (q may be r).
All inputs are finite; a program needn't handle non-finite values.
Results may differ from a plain program's by a relative error of at most 0.00021.
Values sent between devices are 32-bit elements; how exact they have to be, the bound alone decides.
A program may use at most 64 MiB of HBM per device.

v0:
```python
import jax
import jax.numpy as jnp
from jax import lax
from jax.sharding import PartitionSpec as P

BPA = 2
NBD = 4
NG = 8
ITERS = 2


step_scale = 0.08
highest = lax.Precision.HIGHEST


def pick_blocks(bnd_table, indices, commodities, count, block_width):
    return jnp.take(bnd_table.reshape(commodities, count, block_width), indices, axis=1)


def body(
    cost,
    flow_start,
    capacity,
    cap_dual_start,
    demand,
    node_dual_start,
    incidence,
    block_node,
    ghost_source,
):
    commodities, arc_count = cost.shape
    block_count, block_width, _ = incidence.shape
    own_blocks = demand.shape[1] // block_width
    region_total = lax.axis_size("region")
    bound_all = region_total * NBD
    slot_count = own_blocks + NG
    cost_sq = jnp.sum(cost * cost)
    demand_sq = jnp.sum(demand * demand)
    capacity_sq = jnp.sum(capacity * capacity)
    cost_all, demand_all = lax.psum((cost_sq, demand_sq), ("region", "comm"))
    capacity_all = lax.psum(capacity_sq, "region")
    weight = jnp.sqrt(cost_all / (demand_all + capacity_all))
    primal_step = step_scale / weight
    dual_step = step_scale * weight
    slot_table = (block_node[:, None] == jnp.arange(slot_count, dtype=jnp.int32)[None, :]).astype(
        jnp.float32
    )
    ghost_table = (ghost_source[:, None] == jnp.arange(bound_all, dtype=jnp.int32)[None, :]).astype(
        jnp.float32
    )
    flow_now, cap_dual, node_dual = (flow_start, cap_dual_start, node_dual_start)
    edge_cols = NBD * block_width
    for iteration in range(ITERS):
        bnd_table = lax.all_gather(node_dual[:, :edge_cols], "region", axis=1, tiled=True)
        ghost_duals = pick_blocks(bnd_table, ghost_source, commodities, bound_all, block_width)
        dual_blocks = jnp.concatenate(
            [node_dual.reshape(commodities, own_blocks, block_width), ghost_duals], axis=1
        )
        chosen_duals = jnp.take(dual_blocks, block_node, axis=1)
        back_term = jnp.einsum("kbn,bna->kba", chosen_duals, incidence, precision=highest)
        back_term = (
            back_term.reshape(commodities, block_count // BPA, BPA, block_width)
            .sum(axis=2)
            .reshape(commodities, arc_count)
        )
        flow_new = jnp.maximum(flow_now - primal_step * (cost - back_term + cap_dual[None, :]), 0.0)
        flow_bar = 2.0 * flow_new - flow_now
        arc_load = jnp.sum(flow_bar, axis=0)
        load_total = lax.psum(arc_load, "comm")
        cap_dual = jnp.maximum(cap_dual + dual_step * (load_total - capacity), 0.0)
        repeated_flow = jnp.repeat(
            flow_bar.reshape(commodities, arc_count // block_width, block_width), BPA, axis=1
        )
        forward = jnp.einsum("kba,bna->kbn", repeated_flow, incidence, precision=highest)
        slot_rows = jnp.einsum("kbn,bs->ksn", forward, slot_table, precision=highest)
        own_rows = slot_rows[:, :own_blocks]
        routed = jnp.einsum(
            "kgn,gb->kbn", slot_rows[:, own_blocks:], ghost_table, precision=highest
        )
        arrived = lax.psum_scatter(routed, "region", scatter_dimension=1, tiled=True)
        node_rows = jnp.concatenate([own_rows[:, :NBD] + arrived, own_rows[:, NBD:]], axis=1)
        node_dual = node_dual + dual_step * (
            demand - node_rows.reshape(commodities, own_blocks * block_width)
        )
        flow_now = flow_new
    return (flow_now, cap_dual, node_dual)


def solution(mesh):
    return jax.shard_map(
        body,
        mesh=mesh,
        in_specs=(
            P("comm", "region"),
            P("comm", "region"),
            P("region"),
            P("region"),
            P("comm", "region"),
            P("comm", "region"),
            P("region", None, None),
            P("region"),
            P("region"),
        ),
        out_specs=(P("comm", "region"), P("region"), P("comm", "region")),
        check_vma=False,
    )
```

profile of v0, /device:TPU:8, one launch (start us, length us, event | category | flops | bytes accessed | tf_op | source)
XLA Modules:
  0.0 738.6 jit_solution(913210635620972559)
XLA Ops:
  7.2 1.5 slice.30
  8.8 1.6 multiply_reduce_fusion.1
  10.4 1.8 multiply_reduce_fusion
  12.2 1.4 multiply_reduce_fusion.2
  13.6 79.2 %all-reduce = (f32[]{:T(128)}, f32[]{:T(128)}) all-reduce(f32[]{:T(128)} %multiply_reduce_fusion, f32[]{:T(128)} %multiply_reduce_fusion.1), channel_id=1, replica_groups=mesh['region'=32,'comm'=8] {'region','comm'}, use_global_device_ids=true, to_apply=%region_1.0 | all-reduce | flops 2 | bytes 16 | tf_op jit(solution)/shard_map/psum | solution.py:40
  92.9 73.2 %psum.37 = f32[]{:T(128)} all-reduce(f32[]{:T(128)} %multiply_reduce_fusion.2), channel_id=1, replica_groups=mesh['region'=32,'comm'=8] {'region'}, use_global_device_ids=true, to_apply=%region_5.0 | all-reduce | flops 1 | bytes 8 | tf_op jit(solution)/shard_map/psum | solution.py:41
  170.8 1.0 copy_bitcast_fusion.5
  171.8 1.3 copy_bitcast_fusion.1
  174.6 9.6 %bitcast_reduce_fusion.1 = f32[16,64,128]{2,0,1:T(8,128)S(1)} fusion(f32[128,128,128]{2,1,0:T(8,128)} %param.19, f32[128,16,128]{2,1,0:T(8,128)S(1)} %gather_fusion.1, pred[128]{0:T(512)(128)(4,1)S(1)} %compare_and_fusion), kind=kOutput, calls=%fused_computation.13 | convolution fusion | flops 403046400 | bytes 9961600 | tf_op jit(solution)/shard_map/kbn,bna->kba/dot_general | solution.py:60
  184.7 15.4 %convolution_bitcast_fusion.1 = f32[16,128,128]{2,0,1:T(8,128)S(1)} fusion(f32[16,128,128]{2,0,1:T(8,128)S(1)} %bitcast.122, f32[128,128,128]{2,1,0:T(8,128)} %param.19), kind=kOutput, calls=%fused_computation.5 | convolution fusion | flops 402653184 | bytes 10485760 | tf_op jit(solution)/shard_map/kba,bna->kbn/dot_general | solution.py:74
  200.1 0.8 convolution_bitcast_fusion.5
  201.6 1.6 copy.37
  203.3 206.3 %reduce-scatter.3.cloned.1.call-done = f32[16,4,128]{2,0,1:T(8,128)} async-done(((f32[16,128,128]{2,0,1:T(8,128)}), f32[16,4,128]{2,0,1:T(8,128)}) %reduce-scatter.3.cloned.1.call-update) | async-done | bytes 32784 | tf_op jit(solution)/shard_map/reduce_scatter | solution.py:80
  409.6 0.8 slice_add_fusion.1
  411.3 20.9 %psum.38 = f32[8192]{0:T(1024)S(1)} all-reduce(f32[8192]{0:T(1024)S(1)} %get-tuple-element.9), channel_id=1, replica_groups=mesh['region'=32,'comm'=8] {'comm'}, use_global_device_ids=true, to_apply=%region_10.13 | all-reduce | flops 8192 | bytes 65536 | tf_op jit(solution)/shard_map/psum | solution.py:69
  432.2 55.1 %all-gather.5.cloned.1.call-done = f32[16,16384]{1,0:T(8,128)} async-done(((f32[16,512]{1,0:T(8,128)}), f32[16,16384]{1,0:T(8,128)}) %all-gather.5.cloned.1.call-update) | async-done | bytes 1048592 | tf_op jit(solution)/shard_map/all_gather | solution.py:54
  487.3 1.3 copy_bitcast_fusion
  490.1 9.6 %bitcast_reduce_fusion = f32[16,64,128]{2,0,1:T(8,128)S(1)} fusion(f32[128,128,128]{2,1,0:T(8,128)} %param.19, f32[128,16,128]{2,1,0:T(8,128)S(1)} %gather_fusion.3, pred[128]{0:T(512)(128)(4,1)S(1)} %compare_and_fusion), kind=kOutput, calls=%fused_computation.12 | convolution fusion | flops 403046400 | bytes 9961600 | tf_op jit(solution)/shard_map/kbn,bna->kba/dot_general | solution.py:60
  500.0 15.4 %convolution_bitcast_fusion = f32[16,128,128]{2,0,1:T(8,128)S(1)} fusion(f32[16,128,128]{2,0,1:T(8,128)S(1)} %bitcast.123, f32[128,128,128]{2,1,0:T(8,128)} %param.19), kind=kOutput, calls=%fused_computation.4 | convolution fusion | flops 402653184 | bytes 10485760 | tf_op jit(solution)/shard_map/kba,bna->kbn/dot_general | solution.py:74
  516.9 1.6 copy.44
  518.7 20.7 %psum.39 = f32[8192]{0:T(1024)S(1)} all-reduce(f32[8192]{0:T(1024)S(1)} %fusion.31), channel_id=1, replica_groups=mesh['region'=32,'comm'=8] {'comm'}, use_global_device_ids=true, to_apply=%region_12.15 | all-reduce | flops 8192 | bytes 65536 | tf_op jit(solution)/shard_map/psum | solution.py:69
  540.0 190.4 %reduce-scatter.5.cloned.1.call-done = f32[16,4,128]{2,0,1:T(8,128)} async-done(((f32[16,128,128]{2,0,1:T(8,128)}), f32[16,4,128]{2,0,1:T(8,128)}) %reduce-scatter.5.cloned.1.call-update) | async-done | bytes 32784 | tf_op jit(solution)/shard_map/reduce_scatter | solution.py:80
  730.3 0.8 slice_add_fusion
  731.1 0.9 fusion.25
  (60 shorter events, 10.2 us)
Async XLA Ops:
  7.2 177.0 %copy-start = (f32[16,8192]{1,0:T(8,128)S(1)}, f32[16,8192]{1,0:T(8,128)}, u32[]{:S(2)}) copy-start(f32[16,8192]{1,0:T(8,128)} %param.13) | copy-start | bytes 1572868
  7.2 177.0 %copy-start.6 = (f32[8192]{0:T(1024)S(1)}, f32[8192]{0:T(1024)}, u32[]{:S(2)}) copy-start(f32[8192]{0:T(1024)} %param.16) | copy-start | bytes 98308
  7.2 177.0 %copy-start.2 = (f32[16,8192]{1,0:T(8,128)S(1)}, f32[16,8192]{1,0:T(8,128)}, u32[]{:S(2)}) copy-start(f32[16,8192]{1,0:T(8,128)} %param.14) | copy-start | bytes 1572868
  7.2 164.6 %all-gather.3.cloned.1.call-start = ((), (), s32[]{:S(2)}) async-start(), calls=%async_computation.2 | async-start | bytes 1081344 | tf_op jit(solution)/shard_map/all_gather | solution.py:54
  8.7 400.9 %reduce-scatter.3.cloned.1.call-start = ((), (), s32[]{:S(2)}) async-start(), calls=%async_computation.3 | async-start | bytes 1081344 | tf_op jit(solution)/shard_map/reduce_scatter | solution.py:80
  184.2 15.9 %copy-start.7 = (s32[128]{0:T(128)S(1)}, s32[128]{0:T(128)}, u32[]{:S(2)}) copy-start(s32[128]{0:T(128)} %param.20) | copy-start | bytes 1540
  184.2 16.6 %copy-start.8 = (s32[8]{0:T(128)S(1)}, s32[8]{0:T(128)}, u32[]{:S(2)}) copy-start(s32[8]{0:T(128)} %param.21) | copy-start | bytes 100
  184.6 225.8 %copy-start.1 = (f32[16,4096]{1,0:T(8,128)S(1)}, f32[16,4096]{1,0:T(8,128)}, u32[]{:S(2)}) copy-start(f32[16,4096]{1,0:T(8,128)} %param.17) | copy-start | bytes 786436
  184.6 225.8 %copy-start.4 = (f32[16,4096]{1,0:T(8,128)S(1)}, f32[16,4096]{1,0:T(8,128)}, u32[]{:S(2)}) copy-start(f32[16,4096]{1,0:T(8,128)} %param.18) | copy-start | bytes 786436
  184.6 247.5 %copy-start.5 = (f32[8192]{0:T(1024)S(1)}, f32[8192]{0:T(1024)}, u32[]{:S(2)}) copy-start(f32[8192]{0:T(1024)} %param.15) | copy-start | bytes 98308
  203.2 284.1 %all-gather.5.cloned.1.call-start = ((), (), s32[]{:S(2)}) async-start(), calls=%async_computation.4 | async-start | bytes 1081344 | tf_op jit(solution)/shard_map/all_gather | solution.py:54
  411.3 319.1 %reduce-scatter.5.cloned.1.call-start = ((), (), s32[]{:S(2)}) async-start(), calls=%async_computation.5 | async-start | bytes 1081344 | tf_op jit(solution)/shard_map/reduce_scatter | solution.py:80
  499.8 18.7 %copy-start.3 = (f32[16,8192]{1,0:T(8,128)}, f32[16,8192]{1,0:T(8,128)S(1)}, u32[]{:S(2)}) copy-start(f32[16,8192]{1,0:T(8,128)S(1)} %get-tuple-element.8) | copy-start | bytes 1572868
Sparse Core Ops, SparseCore 0:
  11.2 78.9 all-gather.2
  203.3 206.2 reduce-scatter.2
  412.8 74.4 all-gather.4
  518.6 211.6 reduce-scatter.4
where the time goes:
time: 739 us
  waiting for transfers between devices  452 us (61%)
  blocking collectives  194 us (26%)
  matrix products  53 us (7%)
  between operations  16.2 us (2%)
  local copies, waits for them, and re-layouts  11.8 us (2%)
  other arithmetic  11.5 us (2%)
    reduce_scatter x2, waiting for transfers between devices, body(): lax.psum_scatter(routed, 'region', scatter_dimension=1, tiled=True)  397 us
    psum x1, blocking collectives, body(): cost_all, demand_all = lax.psum((cost_sq, demand_sq), ('region', 'comm'))  79.2 us
    psum x1, blocking collectives, body(): capacity_all = lax.psum(capacity_sq, 'region')  73.2 us
    all_gather x2, waiting for transfers between devices, body(): lax.all_gather(node_dual[:, :edge_cols], 'region', axis=1, tiled=True)  55.1 us
    psum x2, blocking collectives, body(): load_total = lax.psum(arc_load, 'comm')  41.5 us
    dot_general x2, matrix products, body(): jnp.einsum('kba,bna->kbn', repeated_flow, incidence, precision=highest)  30.9 us
    dot_general x2, matrix products, body(): jnp.einsum('kbn,bna->kba', chosen_duals, incidence, precision=highest)  19.2 us
  transfers between devices with their start and end apart: 4, of which 3 were waited for; matrix products, arithmetic and copies ran while one was open for 1% of the time, Pallas kernels for 0%

commit v1 on v0

v1 whole, which is shorter than its diff:
```python
import functools

import jax
import jax.numpy as jnp
from jax import lax
from jax.experimental import pallas as pl
from jax.experimental.pallas import tpu as pltpu
from jax.sharding import PartitionSpec as P

BPA = 2
NBD = 4
NG = 8
ITERS = 2
BLK = 128
Z_SIZE = 8
CHUNKS = 8
UNROLL = 8
ROW_PAD = 64

step_scale = 0.08
MESH = pl.DeviceIdType.MESH


def split(value):
    high = value.astype(jnp.bfloat16)
    low = (value - high.astype(jnp.float32)).astype(jnp.bfloat16)
    return high, low


def columns(block):
    if isinstance(block, int):
        return pl.ds(block * BLK, BLK)
    return pl.ds(pl.multiple_of(block * BLK, BLK), BLK)


def square_sum(ref, width):
    def step(index, total):
        for part in range(4):
            piece = ref[:, columns(index * 4 + part)]
            squares = piece * piece
            total = total + (squares[:8] + squares[8:])
        return total

    return lax.fori_loop(0, width // (4 * BLK), step, jnp.zeros((8, BLK), jnp.float32))


def kernel(
    regions,
    comms,
    bn,
    gs,
    bn_row,
    cost,
    flow,
    capacity,
    cap_dual,
    demand,
    node_dual,
    inc_hbm,
    flow_o,
    cap_o,
    nd_o,
    inc_buf,
    w2,
    back_s,
    nd3,
    dtab,
    oh2,
    cand,
    fwd,
    slot,
    rbuf,
    load_s,
    ld_a,
    ld_b,
    sbuf,
    inc_sem,
    sc_send,
    sc_recv,
    gh_send,
    gh_recv,
    rt_send,
    rt_recv,
    ld_send,
    ld_recv,
):
    r = lax.axis_index("region")
    c = lax.axis_index("comm")
    own = nd3.shape[0]
    arc_blocks = w2.shape[0]
    commodities = cost.shape[0]
    x_size = regions // Z_SIZE
    x = r // Z_SIZE
    z = lax.rem(r, Z_SIZE)
    deltas = (1, 2, regions - 2, regions - 1, regions // 2)
    per_chunk = inc_buf.shape[0] // CHUNKS
    load_rows = load_s.shape[0] // comms

    inc_copies = []
    for chunk in range(CHUNKS):
        rows = pl.ds(chunk * per_chunk, per_chunk)
        copy = pltpu.make_async_copy(inc_hbm.at[rows], inc_buf.at[rows], inc_sem.at[chunk])
        copy.start()
        inc_copies.append(copy)

    def comm_peer(off):
        return {"region": r, "comm": lax.rem(c + off, comms)}

    def x_peer(off):
        return {"region": lax.rem(x + off, x_size) * Z_SIZE + z, "comm": c}

    def z_peer(off):
        return {"region": x * Z_SIZE + lax.rem(z + off, Z_SIZE), "comm": c}

    def r_peer(off):
        return {"region": lax.rem(r + off, regions), "comm": c}

    barrier = pltpu.get_barrier_semaphore()
    greeted = 0
    for peer, offs in (
        (comm_peer, range(1, comms)),
        (x_peer, range(1, x_size)),
        (z_peer, range(1, Z_SIZE)),
        (r_peer, deltas[:4]),
    ):
        for off in offs:
            pl.semaphore_signal(barrier, inc=1, device_id=peer(off), device_id_type=MESH)
            greeted += 1

    def spread(index, carry):
        for part in range(4):
            s = index * 4 + part
            value = node_dual[:, columns(s)]
            nd3[s] = value
            high, low = split(value)
            dtab[s, 0:commodities] = high
            dtab[s, commodities:] = low
        return carry

    lax.fori_loop(0, own // 4, spread, 0)
    for j in range(NBD):
        cand[j] = node_dual[:, columns(j)]

    sbuf[0, c, 0:8] = square_sum(cost, cost.shape[1])
    sbuf[0, c, 8:16] = square_sum(demand, demand.shape[1])

    ghost_at = []
    code = bn_row[...]
    slots = code
    for g in range(NG):
        source = gs[g]
        block = source & (NBD - 1)
        delta = lax.rem((source >> 2) - r + regions, regions)
        behind = jnp.maximum(delta - (regions - 5), 3)
        relation = jnp.where(delta <= 2, delta, jnp.where(delta == regions // 2, 5, behind))
        ghost_at.append(relation * NBD + block)
        row = jnp.where(relation == 0, block, own - NBD + relation * NBD + block)
        code = jnp.where(slots == own + g, row, code)
    hits = lax.broadcasted_iota(jnp.int32, (ROW_PAD, BLK), 0) == code
    one_hot = jnp.where(hits, 1.0, 0.0).astype(jnp.bfloat16)
    oh2[:, 0:BLK] = one_hot
    oh2[:, BLK:] = one_hot

    pl.semaphore_wait(barrier, greeted)

    def send_scalars(stage, peer, count, me):
        copies = []
        for off in range(1, count):
            copy = pltpu.make_async_remote_copy(
                src_ref=sbuf.at[stage, me],
                dst_ref=sbuf.at[stage, me],
                send_sem=sc_send.at[stage, off],
                recv_sem=sc_recv.at[stage, off],
                device_id=peer(off),
                device_id_type=MESH,
            )
            copy.start()
            copies.append(copy)
        return copies

    def take_scalars(stage, copies):
        for copy in copies:
            copy.wait()
        total = sbuf[stage, 0]
        for index in range(1, len(copies) + 1):
            total = total + sbuf[stage, index]
        return total

    def send_ghosts(it):
        copies = []
        for index, delta in enumerate(deltas):
            copy = pltpu.make_async_remote_copy(
                src_ref=nd3.at[pl.ds(0, NBD)],
                dst_ref=cand.at[pl.ds(it * 24 + (index + 1) * NBD, NBD)],
                send_sem=gh_send.at[it, index],
                recv_sem=gh_recv.at[it, index],
                device_id=r_peer(regions - delta),
                device_id_type=MESH,
            )
            copy.start()
            copies.append(copy)
        return copies

    def convert(chunk):
        inc_copies[chunk].wait()
        blocks = arc_blocks // CHUNKS

        def step(index, carry):
            a = chunk * blocks + index
            for b in range(BPA):
                high, low = split(inc_buf[a * BPA + b])
                w2[a, b * BLK : (b + 1) * BLK, 0:BLK] = high
                w2[a, b * BLK : (b + 1) * BLK, BLK:] = low
            return carry

        lax.fori_loop(0, blocks, step, 0)

    ghost_copies = send_ghosts(0)
    scalar_copies = send_scalars(0, comm_peer, comms, c)
    for chunk in range(0, 3):
        convert(chunk)
    total = take_scalars(0, scalar_copies)
    cap_sq = jnp.zeros((8, BLK), jnp.float32)
    for part in range(capacity.shape[0] // 8):
        piece = capacity[part * 8 : (part + 1) * 8]
        cap_sq = cap_sq + piece * piece
    sbuf[1, x, 0:8] = total[0:8]
    sbuf[1, x, 8:16] = total[8:16] + cap_sq
    convert(3)
    scalar_copies = send_scalars(1, x_peer, x_size, x)
    for chunk in range(4, 7):
        convert(chunk)
    total = take_scalars(1, scalar_copies)
    sbuf[2, z] = total
    convert(7)
    scalar_copies = send_scalars(2, z_peer, Z_SIZE, z)

    primal_step = None
    dual_step = None
    for it in range(ITERS):
        last = it == ITERS - 1
        flow_src = flow if it == 0 else flow_o
        cap_src = cap_dual if it == 0 else cap_o

        for copy in ghost_copies:
            copy.wait()
        for g in range(NG):
            high, low = split(cand[it * 24 + ghost_at[g]])
            dtab[own + g, 0:commodities] = high
            dtab[own + g, commodities:] = low

        def back_step(index, carry):
            for part in range(UNROLL):
                a = index * UNROLL + part
                left = dtab[bn[a * BPA]]
                right = dtab[bn[a * BPA + 1]]
                product = jnp.dot(
                    jnp.concatenate([left, right], axis=1),
                    w2[a],
                    preferred_element_type=jnp.float32,
                )
                half = product[:commodities] + product[commodities:]
                back_s[:, columns(a)] = half[:, :BLK] + half[:, BLK:]
            return carry

        lax.fori_loop(0, arc_blocks // UNROLL, back_step, 0)

        if it == 0:
            total = take_scalars(2, scalar_copies)
            cost_all = jnp.sum(total[0:8], axis=(0, 1), keepdims=True)
            rest_all = jnp.sum(total[8:16], axis=(0, 1), keepdims=True)
            weight = jnp.sqrt(cost_all / rest_all)
            primal_step = jnp.broadcast_to(step_scale / weight, (1, BLK))
            dual_step = jnp.broadcast_to(step_scale * weight, (1, BLK))
        else:
            finish_load(it - 1)

        def flow_step(index, carry):
            for part in range(UNROLL):
                a = index * UNROLL + part
                now = flow_src[:, columns(a)]
                price = cost[:, columns(a)] - back_s[:, columns(a)] + cap_src[pl.ds(a, 1), :]
                new = jnp.maximum(now - primal_step * price, 0.0)
                bar = 2.0 * new - now
                flow_o[:, columns(a)] = new
                load_s[pl.ds(a, 1), :] = jnp.sum(bar, axis=0, keepdims=True)
                high, low = split(bar)
                terms = jnp.concatenate(
                    [
                        jnp.concatenate([high, high], axis=1),
                        jnp.concatenate([low, low], axis=1),
                    ],
                    axis=0,
                )
                product = lax.dot_general(
                    terms,
                    w2[a],
                    (((1,), (1,)), ((), ())),
                    preferred_element_type=jnp.float32,
                )
                half = product[:commodities] + product[commodities:]
                row = pl.multiple_of(a * (BPA * commodities), BPA * commodities)
                fwd[pl.ds(row, commodities), :] = half[:, :BLK]
                fwd[pl.ds(row + commodities, commodities), :] = half[:, BLK:]
            return carry

        lax.fori_loop(0, arc_blocks // UNROLL, flow_step, 0)

        load_copies = []
        blocks = BPA * arc_blocks
        for pair in range(commodities // 2):
            high_0, low_0 = split(fwd[pl.ds(2 * pair, blocks, stride=commodities), :])
            high_1, low_1 = split(fwd[pl.ds(2 * pair + 1, blocks, stride=commodities), :])
            terms = jnp.concatenate(
                [
                    jnp.concatenate([high_0, high_1], axis=1),
                    jnp.concatenate([low_0, low_1], axis=1),
                ],
                axis=0,
            )
            rows = jnp.dot(oh2[...], terms, preferred_element_type=jnp.float32)
            slot[pl.ds(2 * pair, ROW_PAD, stride=commodities), :] = rows[:, :BLK]
            slot[pl.ds(2 * pair + 1, ROW_PAD, stride=commodities), :] = rows[:, BLK:]
            if pair == 0:
                for off in range(1, comms):
                    target = lax.rem(c + off, comms)
                    copy = pltpu.make_async_remote_copy(
                        src_ref=load_s.at[
                            pl.ds(pl.multiple_of(target * load_rows, load_rows), load_rows)
                        ],
                        dst_ref=ld_a.at[it, c],
                        send_sem=ld_send.at[it, 0, off],
                        recv_sem=ld_recv.at[it, 0, off],
                        device_id=comm_peer(off),
                        device_id_type=MESH,
                    )
                    copy.start()
                    load_copies.append(copy)

        for copy in load_copies:
            copy.wait()
        mine = load_s[pl.ds(pl.multiple_of(c * load_rows, load_rows), load_rows), :]
        for off in range(1, comms):
            mine = mine + ld_a[it, lax.rem(c + off, comms)]
        ld_b[it, c] = mine

        routed_copies = []
        for index, delta in enumerate(deltas):
            rows = NBD * commodities
            copy = pltpu.make_async_remote_copy(
                src_ref=slot.at[pl.ds(own * commodities + index * rows, rows)],
                dst_ref=rbuf.at[it, index],
                send_sem=rt_send.at[it, index],
                recv_sem=rt_recv.at[it, index],
                device_id=r_peer(delta),
                device_id_type=MESH,
            )
            copy.start()
            routed_copies.append(copy)

        total_copies = []
        for off in range(1, comms):
            copy = pltpu.make_async_remote_copy(
                src_ref=ld_b.at[it, c],
                dst_ref=ld_b.at[it, c],
                send_sem=ld_send.at[it, 1, off],
                recv_sem=ld_recv.at[it, 1, off],
                device_id=comm_peer(off),
                device_id_type=MESH,
            )
            copy.start()
            total_copies.append(copy)

        def finish_load(at, copies=total_copies, source=cap_src):
            for copy in copies:
                copy.wait()
            for owner in range(comms):
                rows = slice(owner * load_rows, (owner + 1) * load_rows)
                excess = ld_b[at, owner] - capacity[rows]
                cap_o[rows] = jnp.maximum(source[rows] + dual_step * excess, 0.0)

        def updated(s, rows):
            return nd3[s] + dual_step * (demand[:, columns(s)] - rows)

        def keep(s, value):
            if last:
                nd_o[:, columns(s)] = value
            else:
                nd3[s] = value
                high, low = split(value)
                dtab[s, 0:commodities] = high
                dtab[s, commodities:] = low

        def inner_step(index, carry):
            for part in range(4):
                s = NBD + index * 4 + part
                row = pl.multiple_of(s * commodities, commodities)
                keep(s, updated(s, slot[pl.ds(row, commodities), :]))
            return carry

        lax.fori_loop(0, (own - NBD) // 4, inner_step, 0)

        for copy in routed_copies:
            copy.wait()
        for j in range(NBD):
            rows = slot[j * commodities : (j + 1) * commodities, :]
            for index in range(len(deltas)):
                rows = rows + rbuf[it, index, j * commodities : (j + 1) * commodities, :]
            value = updated(j, rows)
            keep(j, value)
            if not last:
                cand[(it + 1) * 24 + j] = value
        if last:
            finish_load(it)
        else:
            ghost_copies = send_ghosts(it + 1)


def body(
    cost,
    flow_start,
    capacity,
    cap_dual_start,
    demand,
    node_dual_start,
    incidence,
    block_node,
    ghost_source,
):
    regions = lax.axis_size("region")
    comms = lax.axis_size("comm")
    commodities, arcs = cost.shape
    nodes = demand.shape[1]
    arc_blocks = arcs // BLK
    own = nodes // BLK
    blocks = incidence.shape[0]
    f32, bf16 = jnp.float32, jnp.bfloat16
    vmem = pl.BlockSpec(memory_space=pltpu.VMEM)
    smem = pl.BlockSpec(memory_space=pltpu.SMEM)
    dma = pltpu.SemaphoreType.DMA
    relations = 5
    flow_end, cap_end, node_end = pl.pallas_call(
        functools.partial(kernel, regions, comms),
        name="pdhg",
        out_shape=(
            jax.ShapeDtypeStruct((commodities, arcs), f32),
            jax.ShapeDtypeStruct((arc_blocks, BLK), f32),
            jax.ShapeDtypeStruct((commodities, nodes), f32),
        ),
        in_specs=[smem, smem] + [vmem] * 7 + [pl.BlockSpec(memory_space=pl.ANY)],
        out_specs=(vmem, vmem, vmem),
        scratch_shapes=[
            pltpu.VMEM((blocks, BLK, BLK), f32),
            pltpu.VMEM((arc_blocks, BPA * BLK, 2 * BLK), bf16),
            pltpu.VMEM((commodities, arcs), f32),
            pltpu.VMEM((own, commodities, BLK), f32),
            pltpu.VMEM((own + NG, 2 * commodities, BLK), bf16),
            pltpu.VMEM((ROW_PAD, 2 * BLK), bf16),
            pltpu.VMEM((ITERS * 24, commodities, BLK), f32),
            pltpu.VMEM((blocks * commodities, BLK), f32),
            pltpu.VMEM((ROW_PAD * commodities, BLK), f32),
            pltpu.VMEM((ITERS, relations, NBD * commodities, BLK), f32),
            pltpu.VMEM((arc_blocks, BLK), f32),
            pltpu.VMEM((ITERS, comms, arc_blocks // comms, BLK), f32),
            pltpu.VMEM((ITERS, comms, arc_blocks // comms, BLK), f32),
            pltpu.VMEM((3, 8, 16, BLK), f32),
            dma((CHUNKS,)),
            dma((3, 8)),
            dma((3, 8)),
            dma((ITERS, relations)),
            dma((ITERS, relations)),
            dma((ITERS, relations)),
            dma((ITERS, relations)),
            dma((ITERS, 2, 8)),
            dma((ITERS, 2, 8)),
        ],
        compiler_params=pltpu.CompilerParams(
            collective_id=0, has_side_effects=True, vmem_limit_bytes=50 * 1024 * 1024
        ),
    )(
        block_node,
        ghost_source,
        block_node.reshape(1, blocks),
        cost,
        flow_start,
        capacity.reshape(arc_blocks, BLK),
        cap_dual_start.reshape(arc_blocks, BLK),
        demand,
        node_dual_start,
        incidence,
    )
    return flow_end, cap_end.reshape(arcs), node_end


def solution(mesh):
    return jax.shard_map(
        body,
        mesh=mesh,
        in_specs=(
            P("comm", "region"),
            P("comm", "region"),
            P("region"),
            P("region"),
            P("comm", "region"),
            P("comm", "region"),
            P("region", None, None),
            P("region"),
            P("region"),
        ),
        out_specs=(P("comm", "region"), P("region"), P("comm", "region")),
        check_vma=False,
    )
```

time: 739 us -> 68.1 us (0.09)
  the two profiles are of different devices: /device:TPU:8 before, /device:TPU:1 now
where the time goes in v1:
time: 68.1 us; the launch traced here: 67.7 us
  Pallas kernels  58.2 us (85%)
  local copies, waits for them, and re-layouts  8.91 us (13%)
    pallas_call x1, Pallas kernels, body(): pl.pallas_call(functools.partial(kernel, regions, comms), name='pdhg', ou...  58.2 us
    unnamed x19, local copies, waits for them, and re-layouts  8.91 us

profile of v1, /device:TPU:1, one launch (start us, length us, event | category | flops | bytes accessed | tf_op | source)
XLA Modules:
  0.0 67.7 jit_solution(397742918986418026)
XLA Ops:
  0.6 0.0 copy-start
  0.6 1.0 %copy-done = f32[16,8192]{1,0:T(8,128)S(1)} copy-done((f32[16,8192]{1,0:T(8,128)S(1)}, f32[16,8192]{1,0:T(8,128)}, u32[]{:S(2)}) %copy-start) | copy-done | bytes 524312
  1.7 0.0 copy-start.1
  1.7 1.0 %copy-done.1 = f32[16,8192]{1,0:T(8,128)S(1)} copy-done((f32[16,8192]{1,0:T(8,128)S(1)}, f32[16,8192]{1,0:T(8,128)}, u32[]{:S(2)}) %copy-start.1) | copy-done | bytes 524312
  2.7 0.0 copy-start.2
  2.7 0.9 %copy-done.2 = f32[16,4096]{1,0:T(8,128)S(1)} copy-done((f32[16,4096]{1,0:T(8,128)S(1)}, f32[16,4096]{1,0:T(8,128)}, u32[]{:S(2)}) %copy-start.2) | copy-done | bytes 262168
  3.7 0.0 copy-start.3
  3.7 0.9 %copy-done.3 = f32[16,4096]{1,0:T(8,128)S(1)} copy-done((f32[16,4096]{1,0:T(8,128)S(1)}, f32[16,4096]{1,0:T(8,128)}, u32[]{:S(2)}) %copy-start.3) | copy-done | bytes 262168
  4.6 0.0 copy-start.4
  4.6 0.8 %copy-done.4 = f32[8192]{0:T(1024)S(1)} copy-done((f32[8192]{0:T(1024)S(1)}, f32[8192]{0:T(1024)}, u32[]{:S(2)}) %copy-start.4) | copy-done | bytes 32792
  5.4 0.0 copy-start.5
  5.4 0.8 %copy-done.5 = f32[8192]{0:T(1024)S(1)} copy-done((f32[8192]{0:T(1024)S(1)}, f32[8192]{0:T(1024)}, u32[]{:S(2)}) %copy-start.5) | copy-done | bytes 32792
  6.1 0.0 copy-start.6
  6.1 0.7 copy-done.6
  6.8 0.0 copy-start.7
  6.8 0.7 copy-done.7
  7.4 58.2 %pdhg.1 = (f32[16,8192]{1,0:T(8,128)S(1)}, f32[64,128]{1,0:T(8,128)S(1)}, f32[16,4096]{1,0:T(8,128)S(1)}) custom-call(s32[128]{0:T(128)S(1)} %copy-done.6, s32[8]{0:T(128)S(1)} %copy-done.7, s32[1,128]{1,0:T(1,128)S(1)} %bitcast.7, f32[16,8192]{1,0:T(8,128)S(1)} %copy-done, f32[16,8192]{1,0:T(8,128)S(1)} %copy-done.1, f32[64,128]{1,0:T(8,128)S(1)} %bitcast.4, ...), custom_call_target="tpu_custom_call" | custom-call | tf_op jit(solution)/shard_map/pdhg/pallas_call | solution.py:442
  65.6 0.8 %copy.15 = f32[16,8192]{1,0:T(8,128)} copy(f32[16,8192]{1,0:T(8,128)S(1)} %get-tuple-element.12) | data formatting | bytes 1048576
  66.4 0.6 copy.16
  67.0 0.7 %copy.17 = f32[16,4096]{1,0:T(8,128)} copy(f32[16,4096]{1,0:T(8,128)S(1)} %get-tuple-element.14) | data formatting | bytes 524288
Async XLA Ops:
  0.6 1.0 %copy-start = (f32[16,8192]{1,0:T(8,128)S(1)}, f32[16,8192]{1,0:T(8,128)}, u32[]{:S(2)}) copy-start(f32[16,8192]{1,0:T(8,128)} %cost.1) | copy-start | bytes 1572868
  1.7 1.0 %copy-start.1 = (f32[16,8192]{1,0:T(8,128)S(1)}, f32[16,8192]{1,0:T(8,128)}, u32[]{:S(2)}) copy-start(f32[16,8192]{1,0:T(8,128)} %flow.1) | copy-start | bytes 1572868
  2.7 0.9 %copy-start.2 = (f32[16,4096]{1,0:T(8,128)S(1)}, f32[16,4096]{1,0:T(8,128)}, u32[]{:S(2)}) copy-start(f32[16,4096]{1,0:T(8,128)} %demand.1) | copy-start | bytes 786436
  3.7 0.9 %copy-start.3 = (f32[16,4096]{1,0:T(8,128)S(1)}, f32[16,4096]{1,0:T(8,128)}, u32[]{:S(2)}) copy-start(f32[16,4096]{1,0:T(8,128)} %node_dual.1) | copy-start | bytes 786436
  4.6 0.8 %copy-start.4 = (f32[8192]{0:T(1024)S(1)}, f32[8192]{0:T(1024)}, u32[]{:S(2)}) copy-start(f32[8192]{0:T(1024)} %param.11) | copy-start | bytes 98308
  5.4 0.8 %copy-start.5 = (f32[8192]{0:T(1024)S(1)}, f32[8192]{0:T(1024)}, u32[]{:S(2)}) copy-start(f32[8192]{0:T(1024)} %param.12) | copy-start | bytes 98308
  6.1 0.7 copy-start.6
  6.8 0.7 copy-start.7

commit v2 on v1

--- a/solution.py
+++ b/solution.py
@@ -47,6 +47,22 @@
 def kernel(
     regions,
     comms,
+    bn_hbm,
+    gs_hbm,
+    bn_row_hbm,
+    cost_hbm,
+    flow_hbm,
+    capacity_hbm,
+    cap_dual_hbm,
+    demand_hbm,
+    node_dual_hbm,
+    inc_hbm,
+    flow_hbm_o,
+    cap_hbm_o,
+    nd_hbm_o,
+    flow_o,
+    cap_o,
+    nd_o,
     bn,
     gs,
     bn_row,
@@ -56,10 +72,6 @@
     cap_dual,
     demand,
     node_dual,
-    inc_hbm,
-    flow_o,
-    cap_o,
-    nd_o,
     inc_buf,
     w2,
     back_s,
@@ -74,6 +86,8 @@
     ld_a,
     ld_b,
     sbuf,
+    out_sem,
+    arg_sem,
     inc_sem,
     sc_send,
     sc_recv,
@@ -96,6 +110,30 @@
     per_chunk = inc_buf.shape[0] // CHUNKS
     load_rows = load_s.shape[0] // comms
 
+    arg_copies = {}
+    for index, (name, source, target) in enumerate(
+        (
+            ("cost", cost_hbm, cost),
+            ("node_dual", node_dual_hbm, node_dual),
+            ("demand", demand_hbm, demand),
+            ("gs", gs_hbm, gs),
+            ("bn_row", bn_row_hbm, bn_row),
+            ("bn", bn_hbm, bn),
+            ("capacity", capacity_hbm, capacity),
+            ("cap_dual", cap_dual_hbm, cap_dual),
+            ("flow", flow_hbm, flow),
+        )
+    ):
+        copy = pltpu.make_async_copy(source, target, arg_sem.at[index])
+        copy.start()
+        arg_copies[name] = copy
+    out_copies = []
+
+    def put_out(index, source, target):
+        copy = pltpu.make_async_copy(source, target, out_sem.at[index])
+        copy.start()
+        out_copies.append(copy)
+
     inc_copies = []
     for chunk in range(CHUNKS):
         rows = pl.ds(chunk * per_chunk, per_chunk)
@@ -137,13 +175,18 @@
             dtab[s, commodities:] = low
         return carry
 
+    arg_copies["node_dual"].wait()
     lax.fori_loop(0, own // 4, spread, 0)
     for j in range(NBD):
         cand[j] = node_dual[:, columns(j)]
 
+    arg_copies["cost"].wait()
     sbuf[0, c, 0:8] = square_sum(cost, cost.shape[1])
+    arg_copies["demand"].wait()
     sbuf[0, c, 8:16] = square_sum(demand, demand.shape[1])
 
+    arg_copies["gs"].wait()
+    arg_copies["bn_row"].wait()
     ghost_at = []
     code = bn_row[...]
     slots = code
@@ -220,6 +263,7 @@
     for chunk in range(0, 3):
         convert(chunk)
     total = take_scalars(0, scalar_copies)
+    arg_copies["capacity"].wait()
     cap_sq = jnp.zeros((8, BLK), jnp.float32)
     for part in range(capacity.shape[0] // 8):
         piece = capacity[part * 8 : (part + 1) * 8]
@@ -235,6 +279,10 @@
     convert(7)
     scalar_copies = send_scalars(2, z_peer, Z_SIZE, z)
 
+    arg_copies["bn"].wait()
+    arg_copies["cap_dual"].wait()
+    arg_copies["flow"].wait()
+
     primal_step = None
     dual_step = None
     for it in range(ITERS):
@@ -249,42 +297,76 @@
             dtab[own + g, 0:commodities] = high
             dtab[own + g, commodities:] = low
 
+        def back_of(a):
+            left = dtab[bn[a * BPA]]
+            right = dtab[bn[a * BPA + 1]]
+            product = jnp.dot(
+                jnp.concatenate([left, right], axis=1),
+                w2[a],
+                preferred_element_type=jnp.float32,
+            )
+            half = product[:commodities] + product[commodities:]
+            return half[:, :BLK] + half[:, BLK:]
+
+        def update(a, back):
+            now = flow_src[:, columns(a)]
+            price = cost[:, columns(a)] - back + cap_src[pl.ds(a, 1), :]
+            new = jnp.maximum(now - primal_step * price, 0.0)
+            bar = 2.0 * new - now
+            flow_o[:, columns(a)] = new
+            load_s[pl.ds(a, 1), :] = jnp.sum(bar, axis=0, keepdims=True)
+            back_s[:, columns(a)] = bar
+
         def back_step(index, carry):
             for part in range(UNROLL):
                 a = index * UNROLL + part
-                left = dtab[bn[a * BPA]]
-                right = dtab[bn[a * BPA + 1]]
-                product = jnp.dot(
-                    jnp.concatenate([left, right], axis=1),
-                    w2[a],
-                    preferred_element_type=jnp.float32,
-                )
-                half = product[:commodities] + product[commodities:]
-                back_s[:, columns(a)] = half[:, :BLK] + half[:, BLK:]
+                back_s[:, columns(a)] = back_of(a)
             return carry
 
-        lax.fori_loop(0, arc_blocks // UNROLL, back_step, 0)
+        def update_step(index, carry):
+            for part in range(UNROLL):
+                a = index * UNROLL + part
+                update(a, back_s[:, columns(a)])
+            return carry
+
+        def both_step(index, carry):
+            for part in range(UNROLL):
+                a = index * UNROLL + part
+                update(a, back_of(a))
+            return carry
 
         if it == 0:
+            lax.fori_loop(0, arc_blocks // UNROLL, back_step, 0)
             total = take_scalars(2, scalar_copies)
             cost_all = jnp.sum(total[0:8], axis=(0, 1), keepdims=True)
             rest_all = jnp.sum(total[8:16], axis=(0, 1), keepdims=True)
             weight = jnp.sqrt(cost_all / rest_all)
             primal_step = jnp.broadcast_to(step_scale / weight, (1, BLK))
             dual_step = jnp.broadcast_to(step_scale * weight, (1, BLK))
+            lax.fori_loop(0, arc_blocks // UNROLL, update_step, 0)
         else:
-            finish_load(it - 1)
-
-        def flow_step(index, carry):
+            lax.fori_loop(0, arc_blocks // UNROLL, both_step, 0)
+
+        load_copies = []
+        for off in range(1, comms):
+            target = lax.rem(c + off, comms)
+            copy = pltpu.make_async_remote_copy(
+                src_ref=load_s.at[
+                    pl.ds(pl.multiple_of(target * load_rows, load_rows), load_rows)
+                ],
+                dst_ref=ld_a.at[it, c],
+                send_sem=ld_send.at[it, 0, off],
+                recv_sem=ld_recv.at[it, 0, off],
+                device_id=comm_peer(off),
+                device_id_type=MESH,
+            )
+            copy.start()
+            load_copies.append(copy)
+
+        def forward_step(index, carry):
             for part in range(UNROLL):
                 a = index * UNROLL + part
-                now = flow_src[:, columns(a)]
-                price = cost[:, columns(a)] - back_s[:, columns(a)] + cap_src[pl.ds(a, 1), :]
-                new = jnp.maximum(now - primal_step * price, 0.0)
-                bar = 2.0 * new - now
-                flow_o[:, columns(a)] = new
-                load_s[pl.ds(a, 1), :] = jnp.sum(bar, axis=0, keepdims=True)
-                high, low = split(bar)
+                high, low = split(back_s[:, columns(a)])
                 terms = jnp.concatenate(
                     [
                         jnp.concatenate([high, high], axis=1),
@@ -304,9 +386,10 @@
                 fwd[pl.ds(row + commodities, commodities), :] = half[:, BLK:]
             return carry
 
-        lax.fori_loop(0, arc_blocks // UNROLL, flow_step, 0)
-
-        load_copies = []
+        lax.fori_loop(0, arc_blocks // UNROLL, forward_step, 0)
+        if last:
+            put_out(0, flow_o, flow_hbm_o)
+
         blocks = BPA * arc_blocks
         for pair in range(commodities // 2):
             high_0, low_0 = split(fwd[pl.ds(2 * pair, blocks, stride=commodities), :])
@@ -321,28 +404,27 @@
             rows = jnp.dot(oh2[...], terms, preferred_element_type=jnp.float32)
             slot[pl.ds(2 * pair, ROW_PAD, stride=commodities), :] = rows[:, :BLK]
             slot[pl.ds(2 * pair + 1, ROW_PAD, stride=commodities), :] = rows[:, BLK:]
-            if pair == 0:
-                for off in range(1, comms):
-                    target = lax.rem(c + off, comms)
-                    copy = pltpu.make_async_remote_copy(
-                        src_ref=load_s.at[
-                            pl.ds(pl.multiple_of(target * load_rows, load_rows), load_rows)
-                        ],
-                        dst_ref=ld_a.at[it, c],
-                        send_sem=ld_send.at[it, 0, off],
-                        recv_sem=ld_recv.at[it, 0, off],
-                        device_id=comm_peer(off),
-                        device_id_type=MESH,
-                    )
-                    copy.start()
-                    load_copies.append(copy)
-
-        for copy in load_copies:
-            copy.wait()
-        mine = load_s[pl.ds(pl.multiple_of(c * load_rows, load_rows), load_rows), :]
-        for off in range(1, comms):
-            mine = mine + ld_a[it, lax.rem(c + off, comms)]
-        ld_b[it, c] = mine
+
+        def updated(s, rows):
+            return nd3[s] + dual_step * (demand[:, columns(s)] - rows)
+
+        def keep(s, value):
+            if last:
+                nd_o[:, columns(s)] = value
+            else:
+                nd3[s] = value
+                high, low = split(value)
+                dtab[s, 0:commodities] = high
+                dtab[s, commodities:] = low
+
+        def inner_step(index, carry):
+            for part in range(4):
+                s = NBD + index * 4 + part
+                row = pl.multiple_of(s * commodities, commodities)
+                keep(s, updated(s, slot[pl.ds(row, commodities), :]))
+            return carry
+
+        lax.fori_loop(0, 1, inner_step, 0)
 
         routed_copies = []
         for index, delta in enumerate(deltas):
@@ -358,6 +440,17 @@
             copy.start()
             routed_copies.append(copy)
 
+        for copy in load_copies:
+            copy.wait()
+        mine = load_s[pl.ds(pl.multiple_of(c * load_rows, load_rows), load_rows), :]
+        for off in range(1, comms):
+            mine = mine + ld_a[it, lax.rem(c + off, comms)]
+        ld_b[it, c] = mine
+
+        lax.fori_loop(1, (own - NBD) // 4, inner_step, 0)
+        inner = pl.ds(NBD * BLK, (own - NBD) * BLK)
+        edge = pl.ds(0, NBD * BLK)
+
         total_copies = []
         for off in range(1, comms):
             copy = pltpu.make_async_remote_copy(
@@ -379,27 +472,8 @@
                 excess = ld_b[at, owner] - capacity[rows]
                 cap_o[rows] = jnp.maximum(source[rows] + dual_step * excess, 0.0)
 
-        def updated(s, rows):
-            return nd3[s] + dual_step * (demand[:, columns(s)] - rows)
-
-        def keep(s, value):
-            if last:
-                nd_o[:, columns(s)] = value
-            else:
-                nd3[s] = value
-                high, low = split(value)
-                dtab[s, 0:commodities] = high
-                dtab[s, commodities:] = low
-
-        def inner_step(index, carry):
-            for part in range(4):
-                s = NBD + index * 4 + part
-                row = pl.multiple_of(s * commodities, commodities)
-                keep(s, updated(s, slot[pl.ds(row, commodities), :]))
-            return carry
-
-        lax.fori_loop(0, (own - NBD) // 4, inner_step, 0)
-
+        if last:
+            put_out(1, nd_o.at[:, inner], nd_hbm_o.at[:, inner])
         for copy in routed_copies:
             copy.wait()
         for j in range(NBD):
@@ -411,9 +485,14 @@
             if not last:
                 cand[(it + 1) * 24 + j] = value
         if last:
+            put_out(2, nd_o.at[:, edge], nd_hbm_o.at[:, edge])
             finish_load(it)
+            put_out(3, cap_o, cap_hbm_o)
         else:
             ghost_copies = send_ghosts(it + 1)
+            finish_load(it)
+    for copy in out_copies:
+        copy.wait()
 
 
 def body(
@@ -435,8 +514,7 @@
     own = nodes // BLK
     blocks = incidence.shape[0]
     f32, bf16 = jnp.float32, jnp.bfloat16
-    vmem = pl.BlockSpec(memory_space=pltpu.VMEM)
-    smem = pl.BlockSpec(memory_space=pltpu.SMEM)
+    hbm = pl.BlockSpec(memory_space=pltpu.HBM)
     dma = pltpu.SemaphoreType.DMA
     relations = 5
     flow_end, cap_end, node_end = pl.pallas_call(
@@ -447,9 +525,21 @@
             jax.ShapeDtypeStruct((arc_blocks, BLK), f32),
             jax.ShapeDtypeStruct((commodities, nodes), f32),
         ),
-        in_specs=[smem, smem] + [vmem] * 7 + [pl.BlockSpec(memory_space=pl.ANY)],
-        out_specs=(vmem, vmem, vmem),
+        in_specs=[hbm] * 10,
+        out_specs=(hbm, hbm, hbm),
         scratch_shapes=[
+            pltpu.VMEM((commodities, arcs), f32),
+            pltpu.VMEM((arc_blocks, BLK), f32),
+            pltpu.VMEM((commodities, nodes), f32),
+            pltpu.SMEM((blocks,), jnp.int32),
+            pltpu.SMEM((NG,), jnp.int32),
+            pltpu.VMEM((1, blocks), jnp.int32),
+            pltpu.VMEM((commodities, arcs), f32),
+            pltpu.VMEM((commodities, arcs), f32),
+            pltpu.VMEM((arc_blocks, BLK), f32),
+            pltpu.VMEM((arc_blocks, BLK), f32),
+            pltpu.VMEM((commodities, nodes), f32),
+            pltpu.VMEM((commodities, nodes), f32),
             pltpu.VMEM((blocks, BLK, BLK), f32),
             pltpu.VMEM((arc_blocks, BPA * BLK, 2 * BLK), bf16),
             pltpu.VMEM((commodities, arcs), f32),
@@ -464,6 +554,8 @@
             pltpu.VMEM((ITERS, comms, arc_blocks // comms, BLK), f32),
             pltpu.VMEM((ITERS, comms, arc_blocks // comms, BLK), f32),
             pltpu.VMEM((3, 8, 16, BLK), f32),
+            dma((4,)),
+            dma((9,)),
             dma((CHUNKS,)),
             dma((3, 8)),
             dma((3, 8)),
@@ -475,7 +567,7 @@
             dma((ITERS, 2, 8)),
         ],
         compiler_params=pltpu.CompilerParams(
-            collective_id=0, has_side_effects=True, vmem_limit_bytes=50 * 1024 * 1024
+            collective_id=0, has_side_effects=True, vmem_limit_bytes=67_043_328
         ),
     )(
         block_node,

time: 68.1 us -> 56.7 us (0.83)
  the two profiles are of different devices: /device:TPU:1 before, /device:TPU:8 now
where the time goes in v2:
time: 56.7 us; the launch traced here: 56.5 us
  Pallas kernels  51 us (90%)
  local copies, waits for them, and re-layouts  4.91 us (9%)
  between operations  0.64 us (1%)
    pallas_call x1, Pallas kernels, body(): pl.pallas_call(functools.partial(kernel, regions, comms), name='pdhg', ou...  51 us
    unnamed x3, local copies, waits for them, and re-layouts  4.91 us

profile of v2, /device:TPU:8, one launch (start us, length us, event | category | flops | bytes accessed | tf_op | source)
XLA Modules:
  0.0 56.5 jit_solution(6148052571742150642)
XLA Ops:
  0.6 51.0 %pdhg.1 = (f32[16,8192]{1,0:T(8,128)}, f32[64,128]{1,0:T(8,128)}, f32[16,4096]{1,0:T(8,128)}) custom-call(s32[128]{0:T(128)} %bn_hbm.1, s32[8]{0:T(128)} %gs_hbm.1, s32[1,128]{1,0:T(1,128)} %bitcast.7, f32[16,8192]{1,0:T(8,128)} %cost_hbm.1, f32[16,8192]{1,0:T(8,128)} %flow_hbm.1, f32[64,128]{1,0:T(8,128)} %bitcast.4, f32[64,128]{1,0:T(8,128)} %bitcast.5, ...), custom_call_target="tpu_custom_call" | custom-call | tf_op jit(solution)/shard_map/pdhg/pallas_call | solution.py:520
  51.6 1.9 %copy.15 = f32[16,8192]{1,0:T(8,128)} copy(f32[16,8192]{1,0:T(8,128)} %get-tuple-element.12) | data formatting | bytes 1048576
  53.5 1.4 %copy.16 = f32[8192]{0:T(1024)} copy(f32[8192]{0:T(1024)} %bitcast.6) | data formatting | bytes 65536
  54.9 1.7 %copy.17 = f32[16,4096]{1,0:T(8,128)} copy(f32[16,4096]{1,0:T(8,128)} %get-tuple-element.14) | data formatting | bytes 524288

commit v3 on v2

--- a/solution.py
+++ b/solution.py
@@ -57,9 +57,6 @@
     demand_hbm,
     node_dual_hbm,
     inc_hbm,
-    flow_hbm_o,
-    cap_hbm_o,
-    nd_hbm_o,
     flow_o,
     cap_o,
     nd_o,
@@ -86,7 +83,6 @@
     ld_a,
     ld_b,
     sbuf,
-    out_sem,
     arg_sem,
     inc_sem,
     sc_send,
@@ -127,13 +123,6 @@
         copy = pltpu.make_async_copy(source, target, arg_sem.at[index])
         copy.start()
         arg_copies[name] = copy
-    out_copies = []
-
-    def put_out(index, source, target):
-        copy = pltpu.make_async_copy(source, target, out_sem.at[index])
-        copy.start()
-        out_copies.append(copy)
-
     inc_copies = []
     for chunk in range(CHUNKS):
         rows = pl.ds(chunk * per_chunk, per_chunk)
@@ -175,16 +164,73 @@
             dtab[s, commodities:] = low
         return carry
 
+    arg_copies["cost"].wait()
+    sbuf[0, c, 0:8] = square_sum(cost, cost.shape[1])
+    arg_copies["demand"].wait()
+    sbuf[0, c, 8:16] = square_sum(demand, demand.shape[1])
     arg_copies["node_dual"].wait()
     lax.fori_loop(0, own // 4, spread, 0)
     for j in range(NBD):
         cand[j] = node_dual[:, columns(j)]
 
-    arg_copies["cost"].wait()
-    sbuf[0, c, 0:8] = square_sum(cost, cost.shape[1])
-    arg_copies["demand"].wait()
-    sbuf[0, c, 8:16] = square_sum(demand, demand.shape[1])
-
+    pl.semaphore_wait(barrier, greeted)
+
+    def send_scalars(stage, peer, count, me):
+        copies = []
+        for off in range(1, count):
+            copy = pltpu.make_async_remote_copy(
+                src_ref=sbuf.at[stage, me],
+                dst_ref=sbuf.at[stage, me],
+                send_sem=sc_send.at[stage, off],
+                recv_sem=sc_recv.at[stage, off],
+                device_id=peer(off),
+                device_id_type=MESH,
+            )
+            copy.start()
+            copies.append(copy)
+        return copies
+
+    def take_scalars(stage, copies):
+        for copy in copies:
+            copy.wait()
+        total = sbuf[stage, 0]
+        for index in range(1, len(copies) + 1):
+            total = total + sbuf[stage, index]
+        return total
+
+    def send_ghosts(it):
+        copies = []
+        for index, delta in enumerate(deltas):
+            copy = pltpu.make_async_remote_copy(
+                src_ref=nd3.at[pl.ds(0, NBD)],
+                dst_ref=cand.at[pl.ds(it * 24 + (index + 1) * NBD, NBD)],
+                send_sem=gh_send.at[it, index],
+                recv_sem=gh_recv.at[it, index],
+                device_id=r_peer(regions - delta),
+                device_id_type=MESH,
+            )
+            copy.start()
+            copies.append(copy)
+        return copies
+
+    blocks_of = arc_blocks // CHUNKS
+
+    def convert(chunk, first=0, end=blocks_of):
+        if first == 0:
+            inc_copies[chunk].wait()
+
+        def step(index, carry):
+            a = chunk * blocks_of + index
+            for b in range(BPA):
+                high, low = split(inc_buf[a * BPA + b])
+                w2[a, b * BLK : (b + 1) * BLK, 0:BLK] = high
+                w2[a, b * BLK : (b + 1) * BLK, BLK:] = low
+            return carry
+
+        lax.fori_loop(first, end, step, 0)
+
+    scalar_copies = send_scalars(0, comm_peer, comms, c)
+    ghost_copies = send_ghosts(0)
     arg_copies["gs"].wait()
     arg_copies["bn_row"].wait()
     ghost_at = []
@@ -204,80 +250,28 @@
     oh2[:, 0:BLK] = one_hot
     oh2[:, BLK:] = one_hot
 
-    pl.semaphore_wait(barrier, greeted)
-
-    def send_scalars(stage, peer, count, me):
-        copies = []
-        for off in range(1, count):
-            copy = pltpu.make_async_remote_copy(
-                src_ref=sbuf.at[stage, me],
-                dst_ref=sbuf.at[stage, me],
-                send_sem=sc_send.at[stage, off],
-                recv_sem=sc_recv.at[stage, off],
-                device_id=peer(off),
-                device_id_type=MESH,
-            )
-            copy.start()
-            copies.append(copy)
-        return copies
-
-    def take_scalars(stage, copies):
-        for copy in copies:
-            copy.wait()
-        total = sbuf[stage, 0]
-        for index in range(1, len(copies) + 1):
-            total = total + sbuf[stage, index]
-        return total
-
-    def send_ghosts(it):
-        copies = []
-        for index, delta in enumerate(deltas):
-            copy = pltpu.make_async_remote_copy(
-                src_ref=nd3.at[pl.ds(0, NBD)],
-                dst_ref=cand.at[pl.ds(it * 24 + (index + 1) * NBD, NBD)],
-                send_sem=gh_send.at[it, index],
-                recv_sem=gh_recv.at[it, index],
-                device_id=r_peer(regions - delta),
-                device_id_type=MESH,
-            )
-            copy.start()
-            copies.append(copy)
-        return copies
-
-    def convert(chunk):
-        inc_copies[chunk].wait()
-        blocks = arc_blocks // CHUNKS
-
-        def step(index, carry):
-            a = chunk * blocks + index
-            for b in range(BPA):
-                high, low = split(inc_buf[a * BPA + b])
-                w2[a, b * BLK : (b + 1) * BLK, 0:BLK] = high
-                w2[a, b * BLK : (b + 1) * BLK, BLK:] = low
-            return carry
-
-        lax.fori_loop(0, blocks, step, 0)
-
-    ghost_copies = send_ghosts(0)
-    scalar_copies = send_scalars(0, comm_peer, comms, c)
-    for chunk in range(0, 3):
+    for chunk in range(0, 2):
         convert(chunk)
-    total = take_scalars(0, scalar_copies)
     arg_copies["capacity"].wait()
     cap_sq = jnp.zeros((8, BLK), jnp.float32)
     for part in range(capacity.shape[0] // 8):
         piece = capacity[part * 8 : (part + 1) * 8]
         cap_sq = cap_sq + piece * piece
+    total = take_scalars(0, scalar_copies)
     sbuf[1, x, 0:8] = total[0:8]
     sbuf[1, x, 8:16] = total[8:16] + cap_sq
-    convert(3)
+    convert(2, 0, 1)
     scalar_copies = send_scalars(1, x_peer, x_size, x)
-    for chunk in range(4, 7):
+    convert(2, 1)
+    for chunk in range(3, 5):
         convert(chunk)
     total = take_scalars(1, scalar_copies)
     sbuf[2, z] = total
-    convert(7)
+    convert(5, 0, 1)
     scalar_copies = send_scalars(2, z_peer, Z_SIZE, z)
+    convert(5, 1)
+    for chunk in range(6, 8):
+        convert(chunk)
 
     arg_copies["bn"].wait()
     arg_copies["cap_dual"].wait()
@@ -387,8 +381,6 @@
             return carry
 
         lax.fori_loop(0, arc_blocks // UNROLL, forward_step, 0)
-        if last:
-            put_out(0, flow_o, flow_hbm_o)
 
         blocks = BPA * arc_blocks
         for pair in range(commodities // 2):
@@ -448,8 +440,6 @@
         ld_b[it, c] = mine
 
         lax.fori_loop(1, (own - NBD) // 4, inner_step, 0)
-        inner = pl.ds(NBD * BLK, (own - NBD) * BLK)
-        edge = pl.ds(0, NBD * BLK)
 
         total_copies = []
         for off in range(1, comms):
@@ -472,8 +462,6 @@
                 excess = ld_b[at, owner] - capacity[rows]
                 cap_o[rows] = jnp.maximum(source[rows] + dual_step * excess, 0.0)
 
-        if last:
-            put_out(1, nd_o.at[:, inner], nd_hbm_o.at[:, inner])
         for copy in routed_copies:
             copy.wait()
         for j in range(NBD):
@@ -485,13 +473,25 @@
             if not last:
                 cand[(it + 1) * 24 + j] = value
         if last:
-            put_out(2, nd_o.at[:, edge], nd_hbm_o.at[:, edge])
             finish_load(it)
-            put_out(3, cap_o, cap_hbm_o)
         else:
             ghost_copies = send_ghosts(it + 1)
             finish_load(it)
-    for copy in out_copies:
+
+
+def settle(count, *refs):
+    sources, targets, sem = refs[:count], refs[count : 2 * count], refs[2 * count]
+    leaving = []
+    for index in range(count):
+        rows = sources[index].shape[0] // 2
+        for part in range(2):
+            at = pl.ds(part * rows, rows)
+            copy = pltpu.make_async_copy(
+                sources[index].at[at], targets[index].at[at], sem.at[index, part]
+            )
+            copy.start()
+            leaving.append(copy)
+    for copy in leaving:
         copy.wait()
 
 
@@ -515,6 +515,7 @@
     blocks = incidence.shape[0]
     f32, bf16 = jnp.float32, jnp.bfloat16
     hbm = pl.BlockSpec(memory_space=pltpu.HBM)
+    vmem = pl.BlockSpec(memory_space=pltpu.VMEM)
     dma = pltpu.SemaphoreType.DMA
     relations = 5
     flow_end, cap_end, node_end = pl.pallas_call(
@@ -526,11 +527,8 @@
             jax.ShapeDtypeStruct((commodities, nodes), f32),
         ),
         in_specs=[hbm] * 10,
-        out_specs=(hbm, hbm, hbm),
+        out_specs=(vmem, vmem, vmem),
         scratch_shapes=[
-            pltpu.VMEM((commodities, arcs), f32),
-            pltpu.VMEM((arc_blocks, BLK), f32),
-            pltpu.VMEM((commodities, nodes), f32),
             pltpu.SMEM((blocks,), jnp.int32),
             pltpu.SMEM((NG,), jnp.int32),
             pltpu.VMEM((1, blocks), jnp.int32),
@@ -554,7 +552,6 @@
             pltpu.VMEM((ITERS, comms, arc_blocks // comms, BLK), f32),
             pltpu.VMEM((ITERS, comms, arc_blocks // comms, BLK), f32),
             pltpu.VMEM((3, 8, 16, BLK), f32),
-            dma((4,)),
             dma((9,)),
             dma((CHUNKS,)),
             dma((3, 8)),
@@ -567,20 +564,35 @@
             dma((ITERS, 2, 8)),
         ],
         compiler_params=pltpu.CompilerParams(
-            collective_id=0, has_side_effects=True, vmem_limit_bytes=67_043_328
+            collective_id=0, has_side_effects=True, vmem_limit_bytes=50_000_000
         ),
     )(
-        block_node,
-        ghost_source,
-        block_node.reshape(1, blocks),
-        cost,
-        flow_start,
-        capacity.reshape(arc_blocks, BLK),
-        cap_dual_start.reshape(arc_blocks, BLK),
-        demand,
-        node_dual_start,
-        incidence,
+        *(
+            pltpu.with_memory_space_constraint(value, pltpu.HBM)
+            for value in (
+                block_node,
+                ghost_source,
+                block_node.reshape(1, blocks),
+                cost,
+                flow_start,
+                capacity.reshape(arc_blocks, BLK),
+                cap_dual_start.reshape(arc_blocks, BLK),
+                demand,
+                node_dual_start,
+                incidence,
+            )
+        )
     )
+    shapes = (flow_end.shape, cap_end.shape, node_end.shape)
+    flow_end, cap_end, node_end = pl.pallas_call(
+        functools.partial(settle, 3),
+        name="settle",
+        out_shape=tuple(jax.ShapeDtypeStruct(shape, f32) for shape in shapes),
+        in_specs=[vmem] * 3,
+        out_specs=(hbm, hbm, hbm),
+        scratch_shapes=[dma((3, 2))],
+        compiler_params=pltpu.CompilerParams(vmem_limit_bytes=1024 * 1024),
+    )(flow_end, cap_end, node_end)
     return flow_end, cap_end.reshape(arcs), node_end
 
 

time: 56.7 us -> 51.6 us (0.910)
  local copies, waits for them, and re-layouts: 4.91 us -> 0 us
    unnamed x3 -> x0, local copies, waits for them, and re-layouts: 4.91 us -> none
    pallas_call x1, Pallas kernels: 51 us -> 50 us  [body(): pl.pallas_call(functools.partial(kernel, regions, comms), name='pdhg', ou...]
    pallas_call x0 -> x1, Pallas kernels: none -> 0.94 us  [body(): pl.pallas_call(functools.partial(settle, 3), name='settle', out_shape=tup...]
where the time goes in v3:
time: 51.6 us; the launch traced here: 51.5 us
  Pallas kernels  50.9 us (99%)
  between operations  0.64 us (1%)
    pallas_call x1, Pallas kernels, body(): pl.pallas_call(functools.partial(kernel, regions, comms), name='pdhg', ou...  50 us

profile of v3, /device:TPU:8, one launch (start us, length us, event | category | flops | bytes accessed | tf_op | source)
XLA Modules:
  0.0 51.5 jit_solution(1380702169532030521)
XLA Ops:
  0.6 50.0 %pdhg.1 = (f32[16,8192]{1,0:T(8,128)S(1)}, f32[64,128]{1,0:T(8,128)S(1)}, f32[16,4096]{1,0:T(8,128)S(1)}) custom-call(s32[128]{0:T(128)} %bn_hbm.1, s32[8]{0:T(128)} %gs_hbm.1, s32[1,128]{1,0:T(1,128)} %bitcast.6, f32[16,8192]{1,0:T(8,128)} %cost_hbm.1, f32[16,8192]{1,0:T(8,128)} %flow_hbm.1, f32[64,128]{1,0:T(8,128)} %bitcast.4, f32[64,128]{1,0:T(8,128)} %bitcast.5, ...), custom_call_target="tpu_custom_call" | custom-call | tf_op jit(solution)/shard_map/pdhg/pallas_call | solution.py:521
  50.6 0.9 %settle.1 = (f32[16,8192]{1,0:T(8,128)}, f32[64,128]{1,0:T(8,128)}, f32[16,4096]{1,0:T(8,128)}) custom-call(f32[16,8192]{1,0:T(8,128)S(1)} %get-tuple-element.9.refs_0_, f32[64,128]{1,0:T(8,128)S(1)} %get-tuple-element.10.refs_1_, f32[16,4096]{1,0:T(8,128)S(1)} %get-tuple-element.11.refs_2_), custom_call_target="tpu_custom_call" | custom-call | tf_op jit(solution)/shard_map/settle/pallas_call | solution.py:587

commit v4 on v3

--- a/solution.py
+++ b/solution.py
@@ -83,6 +83,11 @@
     ld_a,
     ld_b,
     sbuf,
+    pick_out,
+    pick_in,
+    far_out,
+    pick_send,
+    pick_recv,
     arg_sem,
     inc_sem,
     sc_send,
@@ -102,6 +107,7 @@
     x_size = regions // Z_SIZE
     x = r // Z_SIZE
     z = lax.rem(r, Z_SIZE)
+    order = (4, 1, 2, 0, 3)
     deltas = (1, 2, regions - 2, regions - 1, regions // 2)
     per_chunk = inc_buf.shape[0] // CHUNKS
     load_rows = load_s.shape[0] // comms
@@ -200,10 +206,13 @@
 
     def send_ghosts(it):
         copies = []
-        for index, delta in enumerate(deltas):
+        for index in order:
+            delta = deltas[index]
+            far = index == 4 and it > 0
+            count = 1 if far else NBD
             copy = pltpu.make_async_remote_copy(
-                src_ref=nd3.at[pl.ds(0, NBD)],
-                dst_ref=cand.at[pl.ds(it * 24 + (index + 1) * NBD, NBD)],
+                src_ref=far_out if far else nd3.at[pl.ds(0, NBD)],
+                dst_ref=cand.at[pl.ds(it * 24 + (index + 1) * NBD, count)],
                 send_sem=gh_send.at[it, index],
                 recv_sem=gh_recv.at[it, index],
                 device_id=r_peer(regions - delta),
@@ -234,6 +243,7 @@
     arg_copies["gs"].wait()
     arg_copies["bn_row"].wait()
     ghost_at = []
+    ghost_later = []
     code = bn_row[...]
     slots = code
     for g in range(NG):
@@ -243,12 +253,18 @@
         behind = jnp.maximum(delta - (regions - 5), 3)
         relation = jnp.where(delta <= 2, delta, jnp.where(delta == regions // 2, 5, behind))
         ghost_at.append(relation * NBD + block)
-        row = jnp.where(relation == 0, block, own - NBD + relation * NBD + block)
+        ghost_later.append(jnp.where(relation == 5, 5 * NBD, relation * NBD + block))
+        row = jnp.where(
+            relation == 0, block, jnp.where(relation == 5, own, own + block) + (relation - 1) * NBD
+        )
         code = jnp.where(slots == own + g, row, code)
     hits = lax.broadcasted_iota(jnp.int32, (ROW_PAD, BLK), 0) == code
     one_hot = jnp.where(hits, 1.0, 0.0).astype(jnp.bfloat16)
     oh2[:, 0:BLK] = one_hot
     oh2[:, BLK:] = one_hot
+
+    far_block = gs[0] & (NBD - 1)
+    pick_out[...] = jnp.full(pick_out.shape, far_block, jnp.int32).astype(jnp.float32)
 
     for chunk in range(0, 2):
         convert(chunk)
@@ -257,6 +273,15 @@
     for part in range(capacity.shape[0] // 8):
         piece = capacity[part * 8 : (part + 1) * 8]
         cap_sq = cap_sq + piece * piece
+    pick_copy = pltpu.make_async_remote_copy(
+        src_ref=pick_out,
+        dst_ref=pick_in,
+        send_sem=pick_send.at[0],
+        recv_sem=pick_recv.at[0],
+        device_id=r_peer(regions // 2),
+        device_id_type=MESH,
+    )
+    pick_copy.start()
     total = take_scalars(0, scalar_copies)
     sbuf[1, x, 0:8] = total[0:8]
     sbuf[1, x, 8:16] = total[8:16] + cap_sq
@@ -287,7 +312,7 @@
         for copy in ghost_copies:
             copy.wait()
         for g in range(NG):
-            high, low = split(cand[it * 24 + ghost_at[g]])
+            high, low = split(cand[it * 24 + (ghost_later if it else ghost_at)[g]])
             dtab[own + g, 0:commodities] = high
             dtab[own + g, commodities:] = low
 
@@ -419,11 +444,13 @@
         lax.fori_loop(0, 1, inner_step, 0)
 
         routed_copies = []
-        for index, delta in enumerate(deltas):
+        for index in order:
+            delta = deltas[index]
             rows = NBD * commodities
+            count = commodities if index == 4 else rows
             copy = pltpu.make_async_remote_copy(
-                src_ref=slot.at[pl.ds(own * commodities + index * rows, rows)],
-                dst_ref=rbuf.at[it, index],
+                src_ref=slot.at[pl.ds(own * commodities + index * rows, count)],
+                dst_ref=rbuf.at[it, index, pl.ds(0, count)],
                 send_sem=rt_send.at[it, index],
                 recv_sem=rt_recv.at[it, index],
                 device_id=r_peer(delta),
@@ -462,16 +489,24 @@
                 excess = ld_b[at, owner] - capacity[rows]
                 cap_o[rows] = jnp.maximum(source[rows] + dual_step * excess, 0.0)
 
+        if it == 0:
+            pick_copy.wait()
+        picked = pick_in[...]
         for copy in routed_copies:
             copy.wait()
+        far_value = jnp.zeros((commodities, BLK), jnp.float32)
         for j in range(NBD):
             rows = slot[j * commodities : (j + 1) * commodities, :]
-            for index in range(len(deltas)):
+            for index in range(4):
                 rows = rows + rbuf[it, index, j * commodities : (j + 1) * commodities, :]
+            rows = rows + jnp.where(picked == float(j), rbuf[it, 4, 0:commodities, :], 0.0)
             value = updated(j, rows)
             keep(j, value)
             if not last:
                 cand[(it + 1) * 24 + j] = value
+                far_value = jnp.where(picked == float(j), value, far_value)
+        if not last:
+            far_out[0] = far_value
         if last:
             finish_load(it)
         else:
@@ -552,6 +587,11 @@
             pltpu.VMEM((ITERS, comms, arc_blocks // comms, BLK), f32),
             pltpu.VMEM((ITERS, comms, arc_blocks // comms, BLK), f32),
             pltpu.VMEM((3, 8, 16, BLK), f32),
+            pltpu.VMEM((commodities, BLK), f32),
+            pltpu.VMEM((commodities, BLK), f32),
+            pltpu.VMEM((1, commodities, BLK), f32),
+            dma((1,)),
+            dma((1,)),
             dma((9,)),
             dma((CHUNKS,)),
             dma((3, 8)),

time: 51.6 us -> 50.8 us (0.984)
  Pallas kernels: 50.9 us -> 50 us
    pallas_call x1, Pallas kernels: 50 us -> 49.1 us  [body(): pl.pallas_call(functools.partial(kernel, regions, comms), name='pdhg', ou...]
where the time goes in v4:
time: 50.8 us; the launch traced here: 50.7 us
  Pallas kernels  50 us (98%)
  between operations  0.64 us (1%)
    pallas_call x1, Pallas kernels, body(): pl.pallas_call(functools.partial(kernel, regions, comms), name='pdhg', ou...  49.1 us

profile of v4, /device:TPU:8, one launch (start us, length us, event | category | flops | bytes accessed | tf_op | source)
XLA Modules:
  0.0 50.7 jit_solution(14525794152889873694)
XLA Ops:
  0.6 49.1 %pdhg.1 = (f32[16,8192]{1,0:T(8,128)S(1)}, f32[64,128]{1,0:T(8,128)S(1)}, f32[16,4096]{1,0:T(8,128)S(1)}) custom-call(s32[128]{0:T(128)} %bn_hbm.1, s32[8]{0:T(128)} %gs_hbm.1, s32[1,128]{1,0:T(1,128)} %bitcast.6, f32[16,8192]{1,0:T(8,128)} %cost_hbm.1, f32[16,8192]{1,0:T(8,128)} %flow_hbm.1, f32[64,128]{1,0:T(8,128)} %bitcast.4, f32[64,128]{1,0:T(8,128)} %bitcast.5, ...), custom_call_target="tpu_custom_call" | custom-call | tf_op jit(solution)/shard_map/pdhg/pallas_call | solution.py:556
  49.7 0.9 %settle.1 = (f32[16,8192]{1,0:T(8,128)}, f32[64,128]{1,0:T(8,128)}, f32[16,4096]{1,0:T(8,128)}) custom-call(f32[16,8192]{1,0:T(8,128)S(1)} %get-tuple-element.9.refs_0_, f32[64,128]{1,0:T(8,128)S(1)} %get-tuple-element.10.refs_1_, f32[16,4096]{1,0:T(8,128)S(1)} %get-tuple-element.11.refs_2_), custom_call_target="tpu_custom_call" | custom-call | tf_op jit(solution)/shard_map/settle/pallas_call | solution.py:627

commit v5 on v4

--- a/solution.py
+++ b/solution.py
@@ -14,7 +14,7 @@
 BLK = 128
 Z_SIZE = 8
 CHUNKS = 8
-UNROLL = 8
+UNROLL = 32
 ROW_PAD = 64
 
 step_scale = 0.08

time: 50.8 us -> 49 us (0.965)
  Pallas kernels: 50 us -> 47.8 us
    pallas_call x1, Pallas kernels: 49.1 us -> 46.8 us  [body(): pl.pallas_call(functools.partial(kernel, regions, comms), name='pdhg', ou...]
where the time goes in v5:
time: 49 us; the launch traced here: 48.4 us
  Pallas kernels  47.8 us (98%)
  between operations  0.64 us (1%)
    pallas_call x1, Pallas kernels, body(): pl.pallas_call(functools.partial(kernel, regions, comms), name='pdhg', ou...  46.8 us

profile of v5, /device:TPU:8, one launch (start us, length us, event | category | flops | bytes accessed | tf_op | source)
XLA Modules:
  0.0 48.4 jit_solution(9273669454343678905)
XLA Ops:
  0.6 46.8 %pdhg.1 = (f32[16,8192]{1,0:T(8,128)S(1)}, f32[64,128]{1,0:T(8,128)S(1)}, f32[16,4096]{1,0:T(8,128)S(1)}) custom-call(s32[128]{0:T(128)} %bn_hbm.1, s32[8]{0:T(128)} %gs_hbm.1, s32[1,128]{1,0:T(1,128)} %bitcast.6, f32[16,8192]{1,0:T(8,128)} %cost_hbm.1, f32[16,8192]{1,0:T(8,128)} %flow_hbm.1, f32[64,128]{1,0:T(8,128)} %bitcast.4, f32[64,128]{1,0:T(8,128)} %bitcast.5, ...), custom_call_target="tpu_custom_call" | custom-call | tf_op jit(solution)/shard_map/pdhg/pallas_call | solution.py:556
  47.5 0.9 %settle.1 = (f32[16,8192]{1,0:T(8,128)}, f32[64,128]{1,0:T(8,128)}, f32[16,4096]{1,0:T(8,128)}) custom-call(f32[16,8192]{1,0:T(8,128)S(1)} %get-tuple-element.9.refs_0_, f32[64,128]{1,0:T(8,128)S(1)} %get-tuple-element.10.refs_1_, f32[16,4096]{1,0:T(8,128)S(1)} %get-tuple-element.11.refs_2_), custom_call_target="tpu_custom_call" | custom-call | tf_op jit(solution)/shard_map/settle/pallas_call | solution.py:627
